TPU v7x, 32 devices: a whole 2x2x4 slice. The times are simulated.
32 devices in a mesh: band: 4 (over x, core), tr: 4 (over z), tc: 2 (over y).
Axes of the slice: x: 2, y: 2, z: 4, core: 2. Of those that a mesh axis runs over, the one named last changes fastest.
Arguments:
- voltages: bfloat16 [4096, 2, 1024], P(('band', 'tr', 'tc')), parts along dimension 0, may hold values from -4 to 4
Outputs:
- visibilities: bfloat16 [128, 2, 1024, 1024], P(('band', 'tc'), None, 'tr'), parts along dimension 0
There are 4 independent parts, one for each index of `band`. A program takes and returns all parts, laid end to end along the dimension named above; each array names one. Nothing has to cross between parts.
All inputs are finite; a program needn't handle non-finite values.
Results may differ from a plain program's by a relative error of at most 0.0054.
Values may be sent and summed in bfloat16 or wider, within the bound.
No kernel may reach another device: no remote copies, remote signals or barrier semaphores. Data moves between devices by JAX's collectives and lax.ppermute only.
A program may use at most 64 MiB of HBM per device.

v0:
```python
import math
import jax
import jax.numpy as jnp
from jax import lax
from jax.sharding import PartitionSpec as P

FINE = 32
TAPS = 16


def shifted(block, axis, distance):
    devices = range(lax.axis_size(axis))
    route = [(i - distance, i) for i in devices if i - distance in devices]
    return lax.ppermute(block, axis, route)


def filter_taps(tap_total, fine_total):
    length = tap_total * fine_total
    position = jnp.arange(length).astype(jnp.float32)
    offset = (position - (length - 1) / 2.0) / fine_total
    prototype = jnp.sin(math.pi * offset) / (math.pi * offset)
    prototype = prototype / jnp.sqrt(jnp.sum(prototype * prototype))
    return prototype.reshape(tap_total, fine_total)


def fourier_table(fine_total):
    indices = jnp.arange(fine_total).astype(jnp.float32)
    angles = 2.0 * math.pi * jnp.mod(indices[:, None] * indices[None, :], fine_total) / fine_total
    cosine = jnp.cos(angles)
    sine_part = jnp.sin(angles)
    stacked = jnp.stack(
        [jnp.stack([cosine, -sine_part], axis=-1), jnp.stack([sine_part, cosine], axis=-1)], axis=1
    )
    return stacked.reshape(2 * fine_total, 2 * fine_total)


def filterbank(extended, hop_count):
    inputs = extended.shape[3]
    tap_table = filter_taps(TAPS, FINE)
    fourier = fourier_table(FINE)
    weighted = jnp.zeros((hop_count, FINE, 2, inputs), jnp.float32)
    for tap_index in range(TAPS):
        weighted = weighted + tap_table[tap_index][None, :, None, None] * extended[
            tap_index : tap_index + hop_count
        ].astype(jnp.float32)
    spectra = jnp.einsum(
        "sjm,jo->som",
        weighted.reshape(hop_count, 2 * FINE, inputs),
        fourier,
        precision=lax.Precision.HIGHEST,
    )
    return spectra.reshape(hop_count, FINE, 2, inputs).astype(jnp.bfloat16)


def per_device(voltages):
    samples = voltages.shape[0]
    inputs = voltages.shape[2]
    hop_count = samples // FINE
    needed = TAPS - 1
    shift_count = (needed + hop_count - 1) // hop_count
    earlier = []
    for distance in range(1, shift_count + 1):
        take_hops = min(hop_count, needed - (distance - 1) * hop_count)
        portion = voltages[samples - take_hops * FINE :]
        arrived = shifted(portion, ("tr", "tc"), distance)
        earlier = [arrived] + earlier
    extended = jnp.concatenate(earlier + [voltages], axis=0).reshape(
        needed + hop_count, FINE, 2, inputs
    )
    spectra = filterbank(extended, hop_count)
    turned = lax.all_to_all(
        lax.all_to_all(spectra, "tr", split_axis=3, concat_axis=0, tiled=True),
        "tc",
        split_axis=1,
        concat_axis=0,
        tiled=True,
    )
    spectra_total = turned.shape[0]
    swapped = jnp.stack([turned[:, :, 1], -turned[:, :, 0]], axis=2)
    stacked = jnp.stack([turned, swapped], axis=0)
    inverse_total = 1.0 / float(spectra_total)
    product = jnp.einsum(
        "rskci,skcj->krij",
        stacked,
        lax.all_gather(turned, "tr", axis=3, tiled=True),
        preferred_element_type=jnp.float32,
    )
    summed = product * inverse_total
    return summed.astype(jnp.bfloat16)


def solution(mesh):
    in_specs = (P(("band", "tr", "tc"), None, None),)
    out_specs = P(("band", "tc"), None, "tr", None)
    return jax.shard_map(
        per_device, mesh=mesh, in_specs=in_specs, out_specs=out_specs, check_vma=False
    )
```

profile of v0, /device:TPU:0, one launch (start us, length us, event | category | flops | bytes accessed | tf_op | source)
XLA Modules:
  0.0 185.9 jit_solution(17419271201619337630)
XLA Ops:
  6.5 0.0 all-gather.2.cloned.1.call-start
  6.5 4.9 %collective-permute-start.3 = (bf16[128,2,1024]{2,1,0:T(2,128)(2,1)}, bf16[128,2,1024]{2,1,0:T(2,128)(2,1)S(1)}, u32[]{:S(2)}, u32[]{:S(2)}) collective-permute-start(bf16[128,2,1024]{2,1,0:T(2,128)(2,1)} %param.1), channel_id=1, source_target_pairs={{0,1},{1,2},{2,3},{3,4},{4,5},{5,6},{6,7},{8,9},{9,10},{10,11},{11... | collective-permute-start | bytes 1572872 | tf_op jit(solution)/shard_map/ppermute | solution.py:14
  11.5 3.5 %collective-permute-start.2 = (bf16[128,2,1024]{2,1,0:T(2,128)(2,1)}, bf16[128,2,1024]{2,1,0:T(2,128)(2,1)S(1)}, u32[]{:S(2)}, u32[]{:S(2)}) collective-permute-start(bf16[128,2,1024]{2,1,0:T(2,128)(2,1)} %param.1), channel_id=1, source_target_pairs={{0,2},{1,3},{2,4},{3,5},{4,6},{5,7},{8,10},{9,11},{10,12},{11,13},... | collective-permute-start | bytes 1572872 | tf_op jit(solution)/shard_map/ppermute | solution.py:14
  15.0 4.4 %collective-permute-start.1 = (bf16[128,2,1024]{2,1,0:T(2,128)(2,1)}, bf16[128,2,1024]{2,1,0:T(2,128)(2,1)S(1)}, u32[]{:S(2)}, u32[]{:S(2)}) collective-permute-start(bf16[128,2,1024]{2,1,0:T(2,128)(2,1)} %param.1), channel_id=1, source_target_pairs={{0,3},{1,4},{2,5},{3,6},{4,7},{8,11},{9,12},{10,13},{11,14},{12,15... | collective-permute-start | bytes 1572872 | tf_op jit(solution)/shard_map/ppermute | solution.py:14
  19.4 1.3 slice.142
  20.7 2.0 %collective-permute-start = (bf16[96,2,1024]{2,1,0:T(2,128)(2,1)S(1)}, bf16[96,2,1024]{2,1,0:T(2,128)(2,1)S(1)}, u32[]{:S(2)}, u32[]{:S(2)}) collective-permute-start(bf16[96,2,1024]{2,1,0:T(2,128)(2,1)S(1)} %slice.142), channel_id=1, source_target_pairs={{0,4},{1,5},{2,6},{3,7},{8,12},{9,13},{10,14},{11,15},{16,20},{17,... | collective-permute-start | bytes 1179656 | tf_op jit(solution)/shard_map/ppermute | solution.py:14
  22.7 0.6 multiply_reduce_fusion
  24.1 0.2 fusion.10
  24.2 0.1 fusion.14
  24.3 0.1 mul.296
  24.4 0.1 mul.356
  24.5 0.1 mul.352
  24.6 0.1 mul.348
  24.7 0.1 mul.344
  24.8 0.1 mul.340
  24.9 0.1 mul.336
  24.9 0.1 mul.332
  25.0 0.1 mul.328
  25.1 0.1 mul.324
  25.2 0.1 mul.320
  25.3 0.1 mul.316
  25.4 0.1 mul.312
  25.5 0.1 mul.308
  25.6 0.1 mul.304
  25.7 0.1 mul.300
  25.8 0.5 copy.16
  26.2 0.6 reshape.353
  26.9 18.9 %collective-permute-done = bf16[96,2,1024]{2,1,0:T(2,128)(2,1)S(1)} collective-permute-done((bf16[96,2,1024]{2,1,0:T(2,128)(2,1)S(1)}, bf16[96,2,1024]{2,1,0:T(2,128)(2,1)S(1)}, u32[]{:S(2)}, u32[]{:S(2)}) %collective-permute-start) | collective-permute-done | bytes 393248 | tf_op jit(solution)/shard_map/ppermute | solution.py:14
  45.7 0.3 constant_dynamic-update-slice_fusion.1
  46.0 0.0 copy-start.1
  46.0 0.0 collective-permute-done.1
  46.0 0.6 constant_dynamic-update-slice_fusion
  46.6 0.0 collective-permute-done.2
  46.6 0.6 constant_dynamic-update-slice_fusion.2
  47.2 0.0 collective-permute-done.3
  47.3 0.6 constant_dynamic-update-slice_fusion.4
  47.9 0.0 copy-done.1
  47.9 0.4 constant_dynamic-update-slice_fusion.6
  48.3 7.2 %multiply_add_fusion = f32[128,2,1024]{2,1,0:T(2,128)S(1)} fusion(bf16[128,2,1024]{2,1,0:T(2,128)(2,1)S(1)} %copy-done.1, bf16[128,2,1024]{2,1,0:T(2,128)(2,1)S(1)} %collective-permute-done.3, bf16[128,2,1024]{2,1,0:T(2,128)(2,1)S(1)} %collective-permute-done.2, bf16[128,2,1024]{2,1,0:T(2,128)(2,1)S(1)} %collective-permute-done.1, f32[128]{0:T(128)S(1)} %mul.356, ...), kind=kLoop, calls=%fused_computation.7 | loop fusion | flops 12320768 | bytes 9445376 | tf_op jit(solution)/shard_map/add | solution.py:43
  55.5 0.7 add.121
  56.2 1.0 fusion.2
  57.3 0.2 convert_element_type.138
  57.5 1.9 %copy.18 = bf16[4,32,2,1024]{1,2,0,3:T(2,128)(2,1)S(1)} copy(bf16[4,32,2,1024]{3,2,1,0:T(2,128)(2,1)S(1)} %convert_element_type.138) | data formatting | bytes 1048576 | tf_op jit(solution)/shard_map/convert_element_type | solution.py:52
  59.4 2.2 %reshape.354 = bf16[4,2,32768]{2,1,0:T(2,128)(2,1)S(1)} reshape(bf16[1024,4,2,32]{3,2,1,0:T(2,128)(2,1)S(1)} %bitcast.32) | data formatting | bytes 1048576
  61.6 39.0 %all_to_all.36 = bf16[4,2,32768]{2,1,0:T(2,128)(2,1)S(1)} all-to-all(bf16[4,2,32768]{2,1,0:T(2,128)(2,1)S(1)} %reshape.354), channel_id=1, replica_groups=mesh['band'=4,'tr'=4,'tc'=2] {'tr'}, dimensions={0} | all-to-all | bytes 1048576 | tf_op jit(solution)/shard_map/all_to_all | solution.py:72
  100.6 1.1 reshape.355
  101.6 2.8 %copy.30 = bf16[4,32,2,4,256]{4,3,1,2,0:T(4,128)(2,1)S(1)} copy(bf16[4,32,2,4,256]{1,2,0,4,3:T(2,128)(2,1)S(1)} %bitcast.33) | data formatting | bytes 1048576 | tf_op jit(solution)/shard_map/all_to_all | solution.py:72
  104.5 0.1 copy.20
  104.6 0.5 copy.21
  105.1 17.1 %all_to_all.37 = bf16[16,32,2,256]{3,2,0,1:T(2,128)(2,1)S(1)} all-to-all(bf16[16,32,2,256]{3,2,0,1:T(2,128)(2,1)S(1)} %copy.21), channel_id=1, replica_groups=mesh['band'=4,'tr'=4,'tc'=2] {'tc'}, dimensions={1} | all-to-all | bytes 1048576 | tf_op jit(solution)/shard_map/all_to_all | solution.py:71
  122.2 0.3 copy.22
  122.5 1.1 copy.23
  123.6 0.0 copy-start
  123.6 0.0 all-gather.2.cloned.1.call-update
  123.7 1.1 fusion.13
  124.8 0.1 maximum_bitcast_fusion
  124.8 44.1 %all-gather.2.cloned.1.call-done = bf16[32,16,2,1024]{3,0,2,1:T(8,128)(2,1)} async-done(((bf16[32,16,2,256]{3,0,2,1:T(8,128)(2,1)}), bf16[32,16,2,1024]{3,0,2,1:T(8,128)(2,1)}) %all-gather.2.cloned.1.call-update) | async-done | bytes 2097168 | tf_op jit(solution)/shard_map/all_gather | solution.py:85
  168.9 0.0 copy-done
  168.9 10.1 %fusion = bf16[16,2,256,1024]{3,2,1,0:T(8,128)(2,1)} fusion(bf16[32,16,2,1024]{3,0,2,1:T(8,128)(2,1)} %all-gather.2.cloned.1.call-done, bf16[1,32,16,2,256]{4,1,3,2,0:T(8,128)(2,1)S(1)} %maximum_bitcast_fusion, bf16[1,32,16,2,256]{4,1,3,2,0:T(8,128)(2,1)S(1)} %bitcast.36), kind=kOutput, calls=%fused_computation.1 | convolution fusion | flops 1091043328 | bytes 19922944 | tf_op jit(solution)/shard_map/rskci,skcj->krij/dot_general | solution.py:82
  (20 shorter events, 0.1 us)
Async XLA Ops:
  6.5 162.4 %all-gather.2.cloned.1.call-start = ((), (), s32[]{:S(2)}) async-start(), calls=%async_computation.2 | async-start | bytes 2621440 | tf_op jit(solution)/shard_map/all_gather | solution.py:85
  6.5 40.7 %collective-permute-start.3 = (bf16[128,2,1024]{2,1,0:T(2,128)(2,1)}, bf16[128,2,1024]{2,1,0:T(2,128)(2,1)S(1)}, u32[]{:S(2)}, u32[]{:S(2)}) collective-permute-start(bf16[128,2,1024]{2,1,0:T(2,128)(2,1)} %param.1), channel_id=1, source_target_pairs={{0,1},{1,2},{2,3},{3,4},{4,5},{5,6},{6,7},{8,9},{9,10},{10,11},{11... | collective-permute-start | bytes 1572872 | tf_op jit(solution)/shard_map/ppermute | solution.py:14
  11.5 35.2 %collective-permute-start.2 = (bf16[128,2,1024]{2,1,0:T(2,128)(2,1)}, bf16[128,2,1024]{2,1,0:T(2,128)(2,1)S(1)}, u32[]{:S(2)}, u32[]{:S(2)}) collective-permute-start(bf16[128,2,1024]{2,1,0:T(2,128)(2,1)} %param.1), channel_id=1, source_target_pairs={{0,2},{1,3},{2,4},{3,5},{4,6},{5,7},{8,10},{9,11},{10,12},{11,13},... | collective-permute-start | bytes 1572872 | tf_op jit(solution)/shard_map/ppermute | solution.py:14
  15.0 31.1 %collective-permute-start.1 = (bf16[128,2,1024]{2,1,0:T(2,128)(2,1)}, bf16[128,2,1024]{2,1,0:T(2,128)(2,1)S(1)}, u32[]{:S(2)}, u32[]{:S(2)}) collective-permute-start(bf16[128,2,1024]{2,1,0:T(2,128)(2,1)} %param.1), channel_id=1, source_target_pairs={{0,3},{1,4},{2,5},{3,6},{4,7},{8,11},{9,12},{10,13},{11,14},{12,15... | collective-permute-start | bytes 1572872 | tf_op jit(solution)/shard_map/ppermute | solution.py:14
  20.7 25.0 %collective-permute-start = (bf16[96,2,1024]{2,1,0:T(2,128)(2,1)S(1)}, bf16[96,2,1024]{2,1,0:T(2,128)(2,1)S(1)}, u32[]{:S(2)}, u32[]{:S(2)}) collective-permute-start(bf16[96,2,1024]{2,1,0:T(2,128)(2,1)S(1)} %slice.142), channel_id=1, source_target_pairs={{0,4},{1,5},{2,6},{3,7},{8,12},{9,13},{10,14},{11,15},{16,20},{17,... | collective-permute-start | bytes 1179656 | tf_op jit(solution)/shard_map/ppermute | solution.py:14
  46.0 1.9 copy-start.1
  123.6 45.3 %copy-start = (bf16[2,16,16,2,256]{4,1,0,3,2:T(8,128)(2,1)S(1)}, bf16[2,16,16,2,256]{4,1,0,3,2:T(8,128)(2,1)}, u32[]{:S(2)}) copy-start(bf16[2,16,16,2,256]{4,1,0,3,2:T(8,128)(2,1)} %copy.23) | copy-start | bytes 1572868
Sparse Core Ops, SparseCore 0:
  123.8 45.1 all-gather.1
where the time goes:
time: 186 us
  waiting for transfers between devices  63 us (34%)
  blocking collectives  56.1 us (30%)
  local copies, waits for them, and re-layouts  17.3 us (9%)
  starting transfers between devices  14.8 us (8%)
  between operations  14.3 us (8%)
  matrix products  11.2 us (6%)
  other arithmetic  9.29 us (5%)
    all_gather x1, waiting for transfers between devices, per_device(): lax.all_gather(turned, 'tr', axis=3, tiled=True)  44.1 us
    all_to_all x1, blocking collectives, per_device(): lax.all_to_all(spectra, 'tr', split_axis=3, concat_axis=0, tiled=True)  39 us
    ppermute x4, waiting for transfers between devices, shifted(): return lax.ppermute(block, axis, route)  18.9 us
    all_to_all x1, blocking collectives, per_device(): lax.all_to_all(lax.all_to_all(spectra, 'tr', split_axis=3, concat_axis=0,...  17.1 us
    ppermute x4, starting transfers between devices, shifted(): return lax.ppermute(block, axis, route)  14.8 us
    dot_general x1, matrix products, per_device(): jnp.einsum('rskci,skcj->krij', stacked, lax.all_gather(turned, 'tr', axis...  10.1 us
    add x1, other arithmetic, filterbank(): weighted + tap_table[tap_index][None, :, None, None] * extended[tap_index...  7.23 us
  transfers between devices with their start and end apart: 5, of which 2 were waited for; matrix products, arithmetic and copies ran while one was open for 4% of the time, Pallas kernels for 0%

commit v1 on v0

--- a/solution.py
+++ b/solution.py
@@ -6,6 +6,32 @@
 
 FINE = 32
 TAPS = 16
+
+
+def work_both_ways(array, axis, dim, work, out_dim):
+    devices, position, rows = (lax.axis_size(axis), lax.axis_index(axis), array.shape[dim])
+    upward = [(i, (i + 1) % devices) for i in range(devices)]
+    behind = [(b, a) for a, b in upward]
+    lower, upper = (lax.ppermute(array, axis, upward), lax.ppermute(array, axis, behind))
+    made = work(array, position * rows)
+    length = made.shape[out_dim]
+    filled = jnp.zeros(
+        (*made.shape[:out_dim], devices * length, *made.shape[out_dim + 1 :]), made.dtype
+    )
+
+    def put(filled, made, holder):
+        return lax.dynamic_update_slice_in_dim(filled, made, holder * length, axis=out_dim)
+
+    filled = put(filled, made, position)
+    for step in range(1, devices // 2 + 1):
+        below, above = ((position - step) % devices, (position + step) % devices)
+        held = (lower, upper)
+        if step < devices // 2:
+            lower, upper = (lax.ppermute(lower, axis, upward), lax.ppermute(upper, axis, behind))
+        filled = put(filled, work(held[0], below * rows), below)
+        if 2 * step < devices:
+            filled = put(filled, work(held[1], above * rows), above)
+    return filled
 
 
 def shifted(block, axis, distance):
@@ -79,11 +105,14 @@
     swapped = jnp.stack([turned[:, :, 1], -turned[:, :, 0]], axis=2)
     stacked = jnp.stack([turned, swapped], axis=0)
     inverse_total = 1.0 / float(spectra_total)
-    product = jnp.einsum(
-        "rskci,skcj->krij",
-        stacked,
-        lax.all_gather(turned, "tr", axis=3, tiled=True),
-        preferred_element_type=jnp.float32,
+    product = work_both_ways(
+        turned,
+        "tr",
+        3,
+        lambda shard, offset_2: jnp.einsum(
+            "rskci,skcj->krij", stacked, shard, preferred_element_type=jnp.float32
+        ),
+        3,
     )
     summed = product * inverse_total
     return summed.astype(jnp.bfloat16)

time: 186 us -> 171 us (0.919)
  waiting for transfers between devices: 63 us -> 45.9 us
  starting transfers between devices: 14.8 us -> 30.8 us
  blocking collectives: 56.1 us -> 41 us
  between operations: 14.3 us -> 0.95 us
  other arithmetic: 9.29 us -> 17.5 us
  local copies, waits for them, and re-layouts: 17.3 us -> 22.5 us
    all_gather x1 -> x0, waiting for transfers between devices: 44.1 us -> none  [per_device(): lax.all_gather(turned, 'tr', axis=3, tiled=True)]
    ppermute x0 -> x3, waiting for transfers between devices: none -> 20.7 us  [the longest x1 9.41 us: work_both_ways(): lax.ppermute(lower, axis, upward)]
    all_to_all x1 -> x0, blocking collectives: 17.1 us -> none  [per_device(): lax.all_to_all(lax.all_to_all(spectra, 'tr', split_axis=3, concat_axis=0,...]
    all_to_all x0 -> x1, starting transfers between devices: none -> 12.7 us  [per_device(): lax.all_to_all(lax.all_to_all(spectra, 'tr', split_axis=3, concat_axis=0,...]
    convert_element_type x0 -> x1, other arithmetic: none -> 8.37 us  [per_device(): return summed.astype(jnp.bfloat16)]
    all_to_all x0 -> x1, waiting for transfers between devices: none -> 8.01 us  [per_device(): lax.all_to_all(lax.all_to_all(spectra, 'tr', split_axis=3, concat_axis=0,...]
    broadcast_in_dim x0 -> x1, local copies, waits for them, and re-layouts: none -> 4.2 us  [work_both_ways(): jnp.zeros((*made.shape[:out_dim], devices * length, *made.shape[out_dim +...]
    ppermute x0 -> x3, starting transfers between devices: none -> 3.87 us  [the longest x1 3.81 us: work_both_ways(): lax.ppermute(array, axis, behind)]
  transfers between devices with their start and end apart: 5 -> 8, of which waited for: 2 -> 5; matrix products, arithmetic and copies ran while one was open for 4% -> 11% of each run, Pallas kernels for 0% -> 0%
where the time goes in v1:
time: 171 us; the launch traced here: 170 us
  waiting for transfers between devices  45.9 us (27%)
  blocking collectives  41 us (24%)
  starting transfers between devices  30.8 us (18%)
  local copies, waits for them, and re-layouts  22.5 us (13%)
  other arithmetic  17.5 us (10%)
  matrix products  11.6 us (7%)
    all_to_all x1, blocking collectives, per_device(): lax.all_to_all(spectra, 'tr', split_axis=3, concat_axis=0, tiled=True)  41 us
    ppermute x4, waiting for transfers between devices, shifted(): return lax.ppermute(block, axis, route)  17.3 us
    ppermute x4, starting transfers between devices, shifted(): return lax.ppermute(block, axis, route)  14.3 us
    all_to_all x1, starting transfers between devices, per_device(): lax.all_to_all(lax.all_to_all(spectra, 'tr', split_axis=3, concat_axis=0,...  12.7 us
    dot_general x4, matrix products, per_device(): jnp.einsum('rskci,skcj->krij', stacked, shard, preferred_element_type=jnp...  10.5 us
    ppermute x1, waiting for transfers between devices, work_both_ways(): lax.ppermute(lower, axis, upward)  9.41 us
    convert_element_type x1, other arithmetic, per_device(): return summed.astype(jnp.bfloat16)  8.37 us
    add x1, other arithmetic, filterbank(): weighted + tap_table[tap_index][None, :, None, None] * extended[tap_index...  8.17 us
  transfers between devices with their start and end apart: 8, of which 5 were waited for; matrix products, arithmetic and copies ran while one was open for 11% of the time, Pallas kernels for 0%

profile of v1, /device:TPU:0, one launch (start us, length us, event | category | flops | bytes accessed | tf_op | source)
XLA Modules:
  0.0 170.2 jit_solution(11269883623825842210)
XLA Ops:
  0.0 5.9 %collective-permute-start.1 = (bf16[128,2,1024]{2,1,0:T(2,128)(2,1)}, bf16[128,2,1024]{2,1,0:T(2,128)(2,1)S(1)}, u32[]{:S(2)}, u32[]{:S(2)}) collective-permute-start(bf16[128,2,1024]{2,1,0:T(2,128)(2,1)} %param.1), channel_id=1, source_target_pairs={{0,3},{1,4},{2,5},{3,6},{4,7},{8,11},{9,12},{10,13},{11,14},{12,15... | collective-permute-start | bytes 1572872 | tf_op jit(solution)/shard_map/ppermute | solution.py:40
  5.9 3.5 %collective-permute-start.2 = (bf16[128,2,1024]{2,1,0:T(2,128)(2,1)}, bf16[128,2,1024]{2,1,0:T(2,128)(2,1)S(1)}, u32[]{:S(2)}, u32[]{:S(2)}) collective-permute-start(bf16[128,2,1024]{2,1,0:T(2,128)(2,1)} %param.1), channel_id=1, source_target_pairs={{0,2},{1,3},{2,4},{3,5},{4,6},{5,7},{8,10},{9,11},{10,12},{11,13},... | collective-permute-start | bytes 1572872 | tf_op jit(solution)/shard_map/ppermute | solution.py:40
  9.5 3.4 %collective-permute-start.3 = (bf16[128,2,1024]{2,1,0:T(2,128)(2,1)}, bf16[128,2,1024]{2,1,0:T(2,128)(2,1)S(1)}, u32[]{:S(2)}, u32[]{:S(2)}) collective-permute-start(bf16[128,2,1024]{2,1,0:T(2,128)(2,1)} %param.1), channel_id=1, source_target_pairs={{0,1},{1,2},{2,3},{3,4},{4,5},{5,6},{6,7},{8,9},{9,10},{10,11},{11... | collective-permute-start | bytes 1572872 | tf_op jit(solution)/shard_map/ppermute | solution.py:40
  12.9 1.3 slice.142
  14.2 1.4 collective-permute-start
  15.6 0.6 multiply_reduce_fusion
  17.0 0.2 fusion.14
  17.1 0.1 fusion.18
  17.2 0.1 mul.308
  17.3 0.1 mul.312
  17.4 0.1 mul.316
  17.5 0.1 mul.320
  17.6 0.1 mul.324
  17.7 0.1 mul.328
  17.8 0.1 mul.332
  17.9 0.1 mul.336
  17.9 0.1 mul.340
  18.0 0.1 mul.344
  18.1 0.1 mul.348
  18.2 0.1 mul.352
  18.3 0.1 mul.356
  18.4 0.1 mul.360
  18.5 0.1 mul.364
  18.6 0.1 mul.368
  18.7 0.5 copy.25
  19.1 0.6 reshape.359
  19.8 17.3 %collective-permute-done = bf16[96,2,1024]{2,1,0:T(2,128)(2,1)S(1)} collective-permute-done((bf16[96,2,1024]{2,1,0:T(2,128)(2,1)S(1)}, bf16[96,2,1024]{2,1,0:T(2,128)(2,1)S(1)}, u32[]{:S(2)}, u32[]{:S(2)}) %collective-permute-start) | collective-permute-done | bytes 393248 | tf_op jit(solution)/shard_map/ppermute | solution.py:40
  37.0 0.3 constant_dynamic-update-slice_fusion.1
  37.3 0.0 collective-permute-done.1
  37.3 0.6 constant_dynamic-update-slice_fusion
  37.9 0.0 collective-permute-done.2
  37.9 0.6 constant_dynamic-update-slice_fusion.2
  38.5 0.0 collective-permute-done.3
  38.6 0.6 constant_dynamic-update-slice_fusion.4
  39.2 1.4 constant_dynamic-update-slice_fusion.6
  40.6 8.2 %multiply_add_fusion = f32[128,2,1024]{2,1,0:T(2,128)S(1)} fusion(bf16[128,2,1024]{2,1,0:T(2,128)(2,1)} %param.1, bf16[128,2,1024]{2,1,0:T(2,128)(2,1)S(1)} %collective-permute-done.3, bf16[128,2,1024]{2,1,0:T(2,128)(2,1)S(1)} %collective-permute-done.2, bf16[128,2,1024]{2,1,0:T(2,128)(2,1)S(1)} %collective-permute-done.1, f32[128]{0:T(128)S(1)} %mul.368, ...), kind=kLoop, calls=%fused_computation.8 | loop fusion | flops 12320768 | bytes 9445376 | tf_op jit(solution)/shard_map/add | solution.py:69
  48.8 0.7 add.148
  49.5 1.0 fusion
  50.5 0.2 convert_element_type.138
  50.7 1.9 %copy.27 = bf16[4,32,2,1024]{1,2,0,3:T(2,128)(2,1)S(1)} copy(bf16[4,32,2,1024]{3,2,1,0:T(2,128)(2,1)S(1)} %convert_element_type.138) | data formatting | bytes 1048576 | tf_op jit(solution)/shard_map/convert_element_type | solution.py:78
  52.7 2.2 %reshape.360 = bf16[4,2,32768]{2,1,0:T(2,128)(2,1)S(1)} reshape(bf16[1024,4,2,32]{3,2,1,0:T(2,128)(2,1)S(1)} %bitcast.62) | data formatting | bytes 1048576
  54.8 41.0 %all_to_all.36 = bf16[4,2,32768]{2,1,0:T(2,128)(2,1)S(1)} all-to-all(bf16[4,2,32768]{2,1,0:T(2,128)(2,1)S(1)} %reshape.360), channel_id=1, replica_groups=mesh['band'=4,'tr'=4,'tc'=2] {'tr'}, dimensions={0} | all-to-all | bytes 1048576 | tf_op jit(solution)/shard_map/all_to_all | solution.py:98
  95.8 1.1 reshape.361
  96.9 2.8 %copy.48 = bf16[4,32,2,4,256]{4,3,1,2,0:T(4,128)(2,1)S(1)} copy(bf16[4,32,2,4,256]{1,2,0,4,3:T(2,128)(2,1)S(1)} %bitcast.63) | data formatting | bytes 1048576 | tf_op jit(solution)/shard_map/all_to_all | solution.py:98
  99.7 0.1 copy.29
  99.8 1.3 copy.30
  101.2 12.7 %all-to-all-start.1 = ((bf16[16,32,2,256]{3,2,0,1:T(2,128)(2,1)}), bf16[16,32,2,256]{3,2,0,1:T(2,128)(2,1)S(1)}, u32[]{:S(2)}, u32[]{:S(2)}) async-start(bf16[16,32,2,256]{3,2,0,1:T(2,128)(2,1)} %copy.30), calls=%async_computation.1 | async-start | bytes 1048576 | tf_op jit(solution)/shard_map/all_to_all | solution.py:97
  113.8 8.0 %all-to-all-done.1 = bf16[16,32,2,256]{3,2,0,1:T(2,128)(2,1)S(1)} async-done(((bf16[16,32,2,256]{3,2,0,1:T(2,128)(2,1)}), bf16[16,32,2,256]{3,2,0,1:T(2,128)(2,1)S(1)}, u32[]{:S(2)}, u32[]{:S(2)}) %all-to-all-start.1) | async-done | bytes 524320 | tf_op jit(solution)/shard_map/all_to_all | solution.py:97
  121.9 0.3 copy.31
  122.2 0.3 copy.32
  122.5 0.1 collective-permute-start.4
  122.6 3.8 %collective-permute-start.5 = (bf16[32,16,2,256]{3,0,2,1:T(8,128)(2,1)S(1)}, bf16[32,16,2,256]{3,0,2,1:T(8,128)(2,1)S(1)}, u32[]{:S(2)}, u32[]{:S(2)}) collective-permute-start(bf16[32,16,2,256]{3,0,2,1:T(8,128)(2,1)S(1)} %bitcast.56), channel_id=1, source_target_pairs={{2,0},{4,2},{6,4},{0,6},{3,1},{5,3},{7,5},{1,7},{10,8},{12,10},{14... | collective-permute-start | bytes 1572872 | tf_op jit(solution)/shard_map/ppermute | solution.py:15
  126.4 0.1 maximum_bitcast_fusion
  126.4 4.2 %broadcast_in_dim.2 = f32[16,2,256,1024]{3,2,1,0:T(8,128)S(1)} broadcast(f32[]{:T(128)} %constant.49.clone.1), dimensions={} | broadcast | bytes 33554436 | tf_op jit(solution)/shard_map/broadcast_in_dim | solution.py:18
  130.6 2.6 %bitcast_dynamic-update-slice_fusion.3 = f32[16,2,256,1024]{3,2,1,0:T(8,128)S(1)} fusion(f32[16,2,256,1024]{3,2,1,0:T(8,128)S(1)} %broadcast_in_dim.2, s32[]{:T(128)S(6)} %select_n.53, bf16[32,16,2,256,1]{3,0,2,4,1:T(8,128)(2,1)S(1)} %bitcast.57, bf16[1,32,16,2,256]{4,1,3,2,0:T(8,128)(2,1)S(1)} %maximum_bitcast_fusion, ...), kind=kOutput, calls=%fused_computation.4 | convolution fusion | flops 268959744 | bytes 9961476 | tf_op jit(solution)/shard_map/rskci,skcj->krij/dot_general | solution.py:112
  133.3 5.9 %collective-permute-done.4 = bf16[32,16,2,256]{3,0,2,1:T(8,128)(2,1)S(1)} collective-permute-done((bf16[32,16,2,256]{3,0,2,1:T(8,128)(2,1)S(1)}, bf16[32,16,2,256]{3,0,2,1:T(8,128)(2,1)S(1)}, u32[]{:S(2)}, u32[]{:S(2)}) %collective-permute-start.4) | collective-permute-done | bytes 524320 | tf_op jit(solution)/shard_map/ppermute | solution.py:15
  139.1 0.0 collective-permute-start.6
  139.1 2.6 %bitcast_dynamic-update-slice_fusion.2 = f32[16,2,256,1024]{3,2,1,0:T(8,128)S(1)} fusion(f32[16,2,256,1024]{3,2,1,0:T(8,128)S(1)} %bitcast_dynamic-update-slice_fusion.3, s32[]{:T(128)S(6)} %select_n.55, bf16[32,16,2,256]{3,0,2,1:T(8,128)(2,1)S(1)} %collective-permute-done.4, bf16[1,32,16,2,256]{4,1,3,2,0:T(8,128)(2,1)S(1)} %maximum_bitcast_fusion, ...), kind=kOutput, calls=%fused_computation.3 | convolution fusion | flops 268959744 | bytes 9961476 | tf_op jit(solution)/shard_map/rskci,skcj->krij/dot_general | solution.py:112
  141.8 5.4 %collective-permute-done.5 = bf16[32,16,2,256]{3,0,2,1:T(8,128)(2,1)S(1)} collective-permute-done((bf16[32,16,2,256]{3,0,2,1:T(8,128)(2,1)S(1)}, bf16[32,16,2,256]{3,0,2,1:T(8,128)(2,1)S(1)}, u32[]{:S(2)}, u32[]{:S(2)}) %collective-permute-start.5) | collective-permute-done | bytes 524320 | tf_op jit(solution)/shard_map/ppermute | solution.py:15
  147.2 2.6 %bitcast_dynamic-update-slice_fusion.1 = f32[16,2,256,1024]{3,2,1,0:T(8,128)S(1)} fusion(f32[16,2,256,1024]{3,2,1,0:T(8,128)S(1)} %bitcast_dynamic-update-slice_fusion.2, s32[]{:T(128)S(6)} %select_n.57, bf16[32,16,2,256]{3,0,2,1:T(8,128)(2,1)S(1)} %collective-permute-done.5, bf16[1,32,16,2,256]{4,1,3,2,0:T(8,128)(2,1)S(1)} %maximum_bitcast_fusion, ...), kind=kOutput, calls=%fused_computation.2 | convolution fusion | flops 268959744 | bytes 9961476 | tf_op jit(solution)/shard_map/rskci,skcj->krij/dot_general | solution.py:112
  149.8 9.4 %collective-permute-done.6 = bf16[32,16,2,256]{3,0,2,1:T(8,128)(2,1)S(1)} collective-permute-done((bf16[32,16,2,256]{3,0,2,1:T(8,128)(2,1)S(1)}, bf16[32,16,2,256]{3,0,2,1:T(8,128)(2,1)S(1)}, u32[]{:S(2)}, u32[]{:S(2)}) %collective-permute-start.6) | collective-permute-done | bytes 524320 | tf_op jit(solution)/shard_map/ppermute | solution.py:30
  159.2 2.6 %bitcast_dynamic-update-slice_fusion = f32[16,2,256,1024]{3,2,1,0:T(8,128)S(1)} fusion(f32[16,2,256,1024]{3,2,1,0:T(8,128)S(1)} %bitcast_dynamic-update-slice_fusion.1, s32[]{:T(128)S(6)} %select_n.59, bf16[32,16,2,256]{3,0,2,1:T(8,128)(2,1)S(1)} %collective-permute-done.6, bf16[1,32,16,2,256]{4,1,3,2,0:T(8,128)(2,1)S(1)} %maximum_bitcast_fusion, ...), kind=kOutput, calls=%fused_computation.1 | convolution fusion | flops 268959744 | bytes 9961476 | tf_op jit(solution)/shard_map/rskci,skcj->krij/dot_general | solution.py:112
  161.9 8.4 %multiply_convert_fusion = bf16[16,2,256,1024]{3,2,1,0:T(8,128)(2,1)} fusion(f32[16,2,256,1024]{3,2,1,0:T(8,128)S(1)} %bitcast_dynamic-update-slice_fusion), kind=kLoop, calls=%fused_computation | loop fusion | flops 16777216 | bytes 50331648 | tf_op jit(solution)/shard_map/convert_element_type | solution.py:118
  (21 shorter events, 0.1 us)
Async XLA Ops:
  0.0 37.3 %collective-permute-start.1 = (bf16[128,2,1024]{2,1,0:T(2,128)(2,1)}, bf16[128,2,1024]{2,1,0:T(2,128)(2,1)S(1)}, u32[]{:S(2)}, u32[]{:S(2)}) collective-permute-start(bf16[128,2,1024]{2,1,0:T(2,128)(2,1)} %param.1), channel_id=1, source_target_pairs={{0,3},{1,4},{2,5},{3,6},{4,7},{8,11},{9,12},{10,13},{11,14},{12,15... | collective-permute-start | bytes 1572872 | tf_op jit(solution)/shard_map/ppermute | solution.py:40
  5.9 32.0 %collective-permute-start.2 = (bf16[128,2,1024]{2,1,0:T(2,128)(2,1)}, bf16[128,2,1024]{2,1,0:T(2,128)(2,1)S(1)}, u32[]{:S(2)}, u32[]{:S(2)}) collective-permute-start(bf16[128,2,1024]{2,1,0:T(2,128)(2,1)} %param.1), channel_id=1, source_target_pairs={{0,2},{1,3},{2,4},{3,5},{4,6},{5,7},{8,10},{9,11},{10,12},{11,13},... | collective-permute-start | bytes 1572872 | tf_op jit(solution)/shard_map/ppermute | solution.py:40
  9.5 29.1 %collective-permute-start.3 = (bf16[128,2,1024]{2,1,0:T(2,128)(2,1)}, bf16[128,2,1024]{2,1,0:T(2,128)(2,1)S(1)}, u32[]{:S(2)}, u32[]{:S(2)}) collective-permute-start(bf16[128,2,1024]{2,1,0:T(2,128)(2,1)} %param.1), channel_id=1, source_target_pairs={{0,1},{1,2},{2,3},{3,4},{4,5},{5,6},{6,7},{8,9},{9,10},{10,11},{11... | collective-permute-start | bytes 1572872 | tf_op jit(solution)/shard_map/ppermute | solution.py:40
  14.2 22.8 %collective-permute-start = (bf16[96,2,1024]{2,1,0:T(2,128)(2,1)S(1)}, bf16[96,2,1024]{2,1,0:T(2,128)(2,1)S(1)}, u32[]{:S(2)}, u32[]{:S(2)}) collective-permute-start(bf16[96,2,1024]{2,1,0:T(2,128)(2,1)S(1)} %slice.142), channel_id=1, source_target_pairs={{0,4},{1,5},{2,6},{3,7},{8,12},{9,13},{10,14},{11,15},{16,20},{17,... | collective-permute-start | bytes 1179656 | tf_op jit(solution)/shard_map/ppermute | solution.py:40
  101.2 20.7 %all-to-all-start.1 = ((bf16[16,32,2,256]{3,2,0,1:T(2,128)(2,1)}), bf16[16,32,2,256]{3,2,0,1:T(2,128)(2,1)S(1)}, u32[]{:S(2)}, u32[]{:S(2)}) async-start(bf16[16,32,2,256]{3,2,0,1:T(2,128)(2,1)} %copy.30), calls=%async_computation.1 | async-start | bytes 1048576 | tf_op jit(solution)/shard_map/all_to_all | solution.py:97
  122.5 16.6 %collective-permute-start.4 = (bf16[32,16,2,256]{3,0,2,1:T(8,128)(2,1)S(1)}, bf16[32,16,2,256]{3,0,2,1:T(8,128)(2,1)S(1)}, u32[]{:S(2)}, u32[]{:S(2)}) collective-permute-start(bf16[32,16,2,256]{3,0,2,1:T(8,128)(2,1)S(1)} %bitcast.55), channel_id=1, source_target_pairs={{0,2},{2,4},{4,6},{6,0},{1,3},{3,5},{5,7},{7,1},{8,10},{10,12},{12... | collective-permute-start | bytes 1572872 | tf_op jit(solution)/shard_map/ppermute | solution.py:15
  122.6 24.6 %collective-permute-start.5 = (bf16[32,16,2,256]{3,0,2,1:T(8,128)(2,1)S(1)}, bf16[32,16,2,256]{3,0,2,1:T(8,128)(2,1)S(1)}, u32[]{:S(2)}, u32[]{:S(2)}) collective-permute-start(bf16[32,16,2,256]{3,0,2,1:T(8,128)(2,1)S(1)} %bitcast.56), channel_id=1, source_target_pairs={{2,0},{4,2},{6,4},{0,6},{3,1},{5,3},{7,5},{1,7},{10,8},{12,10},{14... | collective-permute-start | bytes 1572872 | tf_op jit(solution)/shard_map/ppermute | solution.py:15
  139.1 20.1 %collective-permute-start.6 = (bf16[32,16,2,256]{3,0,2,1:T(8,128)(2,1)S(1)}, bf16[32,16,2,256]{3,0,2,1:T(8,128)(2,1)S(1)}, u32[]{:S(2)}, u32[]{:S(2)}) collective-permute-start(bf16[32,16,2,256]{3,0,2,1:T(8,128)(2,1)S(1)} %collective-permute-done.4), channel_id=1, source_target_pairs={{0,2},{2,4},{4,6},{6,0},{1,3},{3,5},{5,7},{7,1},{8,10},{10,12},{12... | collective-permute-start | bytes 1572872 | tf_op jit(solution)/shard_map/ppermute | solution.py:30
